TPU v7x, 32 devices: a whole 2x2x4 slice. The times are simulated.
32 devices in a mesh: row: 8 (over y, x, core), col: 4 (over z).
Axes of the slice: x: 2, y: 2, z: 4, core: 2. Of those that a mesh axis runs over, the one named last changes fastest.
Arguments:
- trailing: float32 [6144, 4096], P('row', 'col'), may hold values from -6 to 6
- column_block: bfloat16 [6144, 1024], P('row', 'col'), may hold values from -6 to 6
- row_block: bfloat16 [1024, 4096], P('row', 'col'), may hold values from -0.1875 to 0.1875
- lower_inv: bfloat16 [1024, 1024], replicated, may hold values from -1 to 1, as said below
- upper_inv: bfloat16 [1024, 1024], replicated, may hold values from -2 to 2, as said below
Outputs:
- lower_panel: bfloat16 [6144, 1024], P('row', 'col')
- upper_panel: bfloat16 [1024, 4096], P('row', 'col')
- updated: float32 [6144, 4096], P('row', 'col')
Inputs may be any that keep to these rules, and one draw needn't show every extreme that they name: `lower_inv`: lower triangular with ones on the diagonal. `upper_inv`: upper triangular with diagonal entries between 0.5 and 2.
All inputs are finite; a program needn't handle non-finite values.
Results may differ from a plain program's by a relative error of at most 0.0044.
Values may be sent and summed in bfloat16 or wider, within the bound.
A program may use at most 64 MiB of HBM per device.

v0:
```python
import jax
import jax.numpy as jnp
from jax import lax
from jax.sharding import PartitionSpec as P


def on_device(trailing, column_block, row_block, lower_inv, upper_inv):
    col_share = column_block.shape[1]
    row_share = row_block.shape[0]
    col_start = lax.axis_index("col") * col_share
    row_start = lax.axis_index("row") * row_share
    factor = upper_inv
    lower_full = jnp.dot(
        lax.all_gather(column_block, "col", axis=1, tiled=True),
        factor,
        preferred_element_type=jnp.float32,
    ).astype(jnp.bfloat16)
    factor = lower_inv
    upper_full = jnp.dot(
        factor,
        lax.all_gather(row_block, "row", axis=0, tiled=True),
        preferred_element_type=jnp.float32,
    ).astype(jnp.bfloat16)
    product = jnp.dot(lower_full, upper_full, preferred_element_type=jnp.float32)
    lower_tile = lax.dynamic_slice_in_dim(lower_full, col_start, col_share, 1)
    upper_tile = lax.dynamic_slice_in_dim(upper_full, row_start, row_share, 0)
    updated = trailing - product
    return (lower_tile, upper_tile, updated)


def solution(mesh):
    in_specs = (P("row", "col"), P("row", "col"), P("row", "col"), P(), P())
    out_specs = (P("row", "col"), P("row", "col"), P("row", "col"))
    return jax.shard_map(
        on_device, mesh=mesh, in_specs=in_specs, out_specs=out_specs, check_vma=False
    )
```

profile of v0, /device:TPU:0, one launch (start us, length us, event | category | flops | bytes accessed | tf_op | source)
XLA Modules:
  0.0 93.0 jit_solution(8704201044639735974)
XLA Ops:
  7.2 0.0 copy-start
  7.2 0.0 all-gather.3.cloned.1.call-start
  7.2 0.7 all-gather.3.cloned.1.call-update
  7.9 0.0 all-gather.5.cloned.1.call-start
  8.0 0.7 all-gather.5.cloned.1.call-update
  8.7 41.3 %all-gather.3.cloned.1.call-done = bf16[768,1024]{1,0:T(8,128)(2,1)} async-done(((bf16[768,256]{1,0:T(8,128)(2,1)}), bf16[768,1024]{1,0:T(8,128)(2,1)}) %all-gather.3.cloned.1.call-update) | async-done | bytes 1572880 | tf_op jit(solution)/shard_map/all_gather | solution.py:14
  50.0 3.9 %convolution_convert_fusion.1 = bf16[768,1024]{1,0:T(8,128)(2,1)S(1)} fusion(bf16[768,1024]{1,0:T(8,128)(2,1)} %all-gather.3.cloned.1.call-done, bf16[1024,1024]{1,0:T(8,128)(2,1)} %param.9), kind=kOutput, calls=%fused_computation.2 | convolution fusion | flops 1611399168 | bytes 5242880 | tf_op jit(solution)/shard_map/dot_general | solution.py:13
  53.9 0.0 copy-start.1
  53.9 1.1 %copy-done.1 = bf16[768,1024]{1,0:T(8,128)(2,1)} copy-done((bf16[768,1024]{1,0:T(8,128)(2,1)}, bf16[768,1024]{1,0:T(8,128)(2,1)S(1)}, u32[]{:S(2)}) %copy-start.1) | copy-done | bytes 1572888
  55.0 0.8 constant_dynamic-slice_fusion.1
  55.8 22.1 %all-gather.5.cloned.1.call-done = bf16[1024,1024]{1,0:T(8,128)(2,1)} async-done(((bf16[128,1024]{1,0:T(8,128)(2,1)}), bf16[1024,1024]{1,0:T(8,128)(2,1)}) %all-gather.5.cloned.1.call-update) | async-done | bytes 2097168 | tf_op jit(solution)/shard_map/all_gather | solution.py:21
  77.9 0.0 copy-done
  77.9 0.0 copy-start.2
  77.9 0.0 copy-start.3
  77.9 4.1 %convolution_convert_fusion = bf16[1024,1024]{1,0:T(8,128)(2,1)S(1)} fusion(bf16[1024,1024]{1,0:T(8,128)(2,1)S(1)} %copy-done, bf16[1024,1024]{1,0:T(8,128)(2,1)} %all-gather.5.cloned.1.call-done), kind=kOutput, calls=%fused_computation | convolution fusion | flops 2148532224 | bytes 6291456 | tf_op jit(solution)/shard_map/dot_general | solution.py:19
  82.0 0.7 constant_dynamic-slice_fusion
  82.7 0.0 copy-done.2
  82.7 0.0 copy-done.3
  82.7 3.5 %convolution_subtract_fusion = f32[768,1024]{1,0:T(8,128)} fusion(f32[768,1024]{1,0:T(8,128)S(1)} %copy-done.3, bf16[768,1024]{1,0:T(8,128)(2,1)S(1)} %copy-done.2, bf16[1024,1024]{1,0:T(8,128)(2,1)S(1)} %convolution_convert_fusion), kind=kOutput, calls=%fused_computation.1 | convolution fusion | flops 1611399168 | bytes 9961472 | tf_op jit(solution)/shard_map/dot_general | solution.py:24
Async XLA Ops:
  7.2 70.8 %copy-start = (bf16[1024,1024]{1,0:T(8,128)(2,1)S(1)}, bf16[1024,1024]{1,0:T(8,128)(2,1)}, u32[]{:S(2)}) copy-start(bf16[1024,1024]{1,0:T(8,128)(2,1)} %param.8) | copy-start | bytes 6291460
  7.2 42.8 %all-gather.3.cloned.1.call-start = ((), (), s32[]{:S(2)}) async-start(), calls=%async_computation | async-start | bytes 1966080 | tf_op jit(solution)/shard_map/all_gather | solution.py:14
  7.9 70.0 %all-gather.5.cloned.1.call-start = ((), (), s32[]{:S(2)}) async-start(), calls=%async_computation.1 | async-start | bytes 2359296 | tf_op jit(solution)/shard_map/all_gather | solution.py:21
  53.9 1.1 %copy-start.1 = (bf16[768,1024]{1,0:T(8,128)(2,1)}, bf16[768,1024]{1,0:T(8,128)(2,1)S(1)}, u32[]{:S(2)}) copy-start(bf16[768,1024]{1,0:T(8,128)(2,1)S(1)} %convolution_convert_fusion.1) | copy-start | bytes 4718596
  77.9 4.8 %copy-start.2 = (bf16[768,1024]{1,0:T(8,128)(2,1)S(1)}, bf16[768,1024]{1,0:T(8,128)(2,1)}, u32[]{:S(2)}) copy-start(bf16[768,1024]{1,0:T(8,128)(2,1)} %copy-done.1) | copy-start | bytes 4718596
  77.9 4.8 %copy-start.3 = (f32[768,1024]{1,0:T(8,128)S(1)}, f32[768,1024]{1,0:T(8,128)}, u32[]{:S(2)}) copy-start(f32[768,1024]{1,0:T(8,128)} %param.5) | copy-start | bytes 9437188
Sparse Core Ops, SparseCore 0:
  9.5 40.3 all-gather.2
  51.9 25.9 all-gather.4
where the time goes:
time: 93.2 us; the launch traced here: 93 us
  waiting for transfers between devices  64.8 us (70%)
  between operations  14.1 us (15%)
  matrix products  11.4 us (12%)
  local copies, waits for them, and re-layouts  2.68 us (3%)
    all_gather x1, waiting for transfers between devices, on_device(): lax.all_gather(column_block, 'col', axis=1, tiled=True)  41.3 us
    all_gather x1, waiting for transfers between devices, on_device(): lax.all_gather(row_block, 'row', axis=0, tiled=True)  22.1 us
    dot_general x1, matrix products, on_device(): jnp.dot(factor, lax.all_gather(row_block, 'row', axis=0, tiled=True), pre...  4.06 us
    dot_general x1, matrix products, on_device(): jnp.dot(lax.all_gather(column_block, 'col', axis=1, tiled=True), factor,...  3.86 us
    dot_general x1, matrix products, on_device(): jnp.dot(lower_full, upper_full, preferred_element_type=jnp.float32)  3.47 us
  transfers between devices with their start and end apart: 2, of which 2 were waited for; matrix products, arithmetic and copies ran while one was open for 5% of the time, Pallas kernels for 0%

commit v1 on v0

--- a/solution.py
+++ b/solution.py
@@ -18,7 +18,9 @@
     factor = lower_inv
     upper_full = jnp.dot(
         factor,
-        lax.all_gather(row_block, "row", axis=0, tiled=True),
+        jnp.concatenate(
+            lax.all_to_all(jnp.stack([row_block] * lax.axis_size("row")), "row", 0, 0), axis=0
+        ),
         preferred_element_type=jnp.float32,
     ).astype(jnp.bfloat16)
     product = jnp.dot(lower_full, upper_full, preferred_element_type=jnp.float32)

time: 93.2 us -> 72.8 us (0.78)
  waiting for transfers between devices: 64.8 us -> 36.3 us
  starting transfers between devices: 0.08 us -> 5.24 us
  local copies, waits for them, and re-layouts: 2.68 us -> 5.54 us
    all_gather x1, waiting for transfers between devices: 41.3 us -> 9.63 us  [on_device(): lax.all_gather(column_block, 'col', axis=1, tiled=True)]
    all_to_all x0 -> x1, waiting for transfers between devices: none -> 26 us  [on_device(): lax.all_to_all(jnp.stack([row_block] * lax.axis_size('row')), 'row', 0, 0)]
    all_gather x1 -> x0, waiting for transfers between devices: 22.1 us -> none  [on_device(): lax.all_gather(row_block, 'row', axis=0, tiled=True)]
    all_to_all x0 -> x1, starting transfers between devices: none -> 5.2 us  [on_device(): lax.all_to_all(jnp.stack([row_block] * lax.axis_size('row')), 'row', 0, 0)]
    another operation x0 -> x1, local copies, waits for them, and re-layouts: none -> 2.68 us  [on_device(): jnp.stack([row_block] * lax.axis_size('row'))]
  transfers between devices with their start and end apart: 2 -> 2, of which waited for: 2 -> 2; matrix products, arithmetic and copies ran while one was open for 5% -> 6% of each run, Pallas kernels for 0% -> 0%
where the time goes in v1:
time: 72.8 us; the launch traced here: 72.5 us
  waiting for transfers between devices  36.3 us (50%)
  between operations  14.1 us (19%)
  matrix products  11.4 us (16%)
  local copies, waits for them, and re-layouts  5.54 us (8%)
  starting transfers between devices  5.24 us (7%)
    all_to_all x1, waiting for transfers between devices, on_device(): lax.all_to_all(jnp.stack([row_block] * lax.axis_size('row')), 'row', 0, 0)  26 us
    all_gather x1, waiting for transfers between devices, on_device(): lax.all_gather(column_block, 'col', axis=1, tiled=True)  9.63 us
    all_to_all x1, starting transfers between devices, on_device(): lax.all_to_all(jnp.stack([row_block] * lax.axis_size('row')), 'row', 0, 0)  5.2 us
    dot_general x1, matrix products, on_device(): jnp.dot(lax.all_gather(column_block, 'col', axis=1, tiled=True), factor,...  4 us
    dot_general x1, matrix products, on_device(): jnp.dot(factor, jnp.concatenate(lax.all_to_all(jnp.stack([row_block] * la...  3.93 us
    dot_general x1, matrix products, on_device(): jnp.dot(lower_full, upper_full, preferred_element_type=jnp.float32)  3.47 us
    another operation x1, local copies, waits for them, and re-layouts, on_device(): jnp.stack([row_block] * lax.axis_size('row'))  2.68 us
  transfers between devices with their start and end apart: 2, of which 2 were waited for; matrix products, arithmetic and copies ran while one was open for 6% of the time, Pallas kernels for 0%

profile of v1, /device:TPU:0, one launch (start us, length us, event | category | flops | bytes accessed | tf_op | source)
XLA Modules:
  0.0 72.5 jit_solution(11361054811743715471)
XLA Ops:
  7.2 0.0 copy-start
  7.2 2.7 %stack.2 = bf16[8,128,1024]{2,1,0:T(8,128)(2,1)} broadcast(bf16[128,1024]{1,0:T(8,128)(2,1)} %param.7), dimensions={1,2} | broadcast | bytes 2359296 | tf_op jit(solution)/shard_map/stack | solution.py:22
  9.9 5.2 %all-to-all-start = ((bf16[8,128,1024]{2,1,0:T(8,128)(2,1)}), bf16[8,128,1024]{2,1,0:T(8,128)(2,1)}, u32[]{:S(2)}, u32[]{:S(2)}) async-start(bf16[8,128,1024]{2,1,0:T(8,128)(2,1)} %stack.2), calls=%async_computation | async-start | bytes 4194304 | tf_op jit(solution)/shard_map/all_to_all | solution.py:22
  15.1 0.0 all-gather.2.cloned.1.call-start
  15.1 0.7 all-gather.2.cloned.1.call-update
  15.8 26.0 %all-to-all-done = bf16[8,128,1024]{2,1,0:T(8,128)(2,1)} async-done(((bf16[8,128,1024]{2,1,0:T(8,128)(2,1)}), bf16[8,128,1024]{2,1,0:T(8,128)(2,1)}, u32[]{:S(2)}, u32[]{:S(2)}) %all-to-all-start) | async-done | bytes 2097184 | tf_op jit(solution)/shard_map/all_to_all | solution.py:22
  41.8 0.0 copy-done
  41.8 3.9 %convolution_convert_fusion = bf16[1024,1024]{1,0:T(8,128)(2,1)S(1)} fusion(bf16[1024,1024]{1,0:T(8,128)(2,1)S(1)} %copy-done, bf16[1024,1024]{1,0:T(8,128)(2,1)} %bitcast), kind=kOutput, calls=%fused_computation | convolution fusion | flops 2148532224 | bytes 6291456 | tf_op jit(solution)/shard_map/dot_general | solution.py:19
  45.7 0.0 copy-start.1
  45.7 1.3 %copy-done.1 = bf16[1024,1024]{1,0:T(8,128)(2,1)} copy-done((bf16[1024,1024]{1,0:T(8,128)(2,1)}, bf16[1024,1024]{1,0:T(8,128)(2,1)S(1)}, u32[]{:S(2)}) %copy-start.1) | copy-done | bytes 2097176
  47.0 0.7 constant_dynamic-slice_fusion
  47.8 9.6 %all-gather.2.cloned.1.call-done = bf16[768,1024]{1,0:T(8,128)(2,1)} async-done(((bf16[768,256]{1,0:T(8,128)(2,1)}), bf16[768,1024]{1,0:T(8,128)(2,1)}) %all-gather.2.cloned.1.call-update) | async-done | bytes 1572880 | tf_op jit(solution)/shard_map/all_gather | solution.py:14
  57.4 0.0 copy-start.2
  57.4 0.0 copy-start.3
  57.4 4.0 %convolution_convert_fusion.1 = bf16[768,1024]{1,0:T(8,128)(2,1)S(1)} fusion(bf16[768,1024]{1,0:T(8,128)(2,1)} %all-gather.2.cloned.1.call-done, bf16[1024,1024]{1,0:T(8,128)(2,1)} %param.9), kind=kOutput, calls=%fused_computation.2 | convolution fusion | flops 1611399168 | bytes 5242880 | tf_op jit(solution)/shard_map/dot_general | solution.py:13
  61.4 0.8 %constant_dynamic-slice_fusion.1 = bf16[768,256]{1,0:T(8,128)(2,1)} fusion(bf16[768,1024]{1,0:T(8,128)(2,1)S(1)} %convolution_convert_fusion.1, s32[]{:T(128)S(6)} %select_n.6), kind=kLoop, calls=%fused_computation.4 | loop fusion | bytes 786436 | tf_op jit(solution)/shard_map/dynamic_slice | solution.py:27
  62.2 0.0 copy-done.2
  62.2 0.0 copy-done.3
  62.2 3.5 %convolution_subtract_fusion = f32[768,1024]{1,0:T(8,128)} fusion(f32[768,1024]{1,0:T(8,128)S(1)} %copy-done.3, bf16[768,1024]{1,0:T(8,128)(2,1)S(1)} %convolution_convert_fusion.1, bf16[1024,1024]{1,0:T(8,128)(2,1)S(1)} %copy-done.2), kind=kOutput, calls=%fused_computation.1 | convolution fusion | flops 1611399168 | bytes 9961472 | tf_op jit(solution)/shard_map/dot_general | solution.py:26
Async XLA Ops:
  7.2 34.6 %copy-start = (bf16[1024,1024]{1,0:T(8,128)(2,1)S(1)}, bf16[1024,1024]{1,0:T(8,128)(2,1)}, u32[]{:S(2)}) copy-start(bf16[1024,1024]{1,0:T(8,128)(2,1)} %param.8) | copy-start | bytes 6291460
  9.9 31.9 %all-to-all-start = ((bf16[8,128,1024]{2,1,0:T(8,128)(2,1)}), bf16[8,128,1024]{2,1,0:T(8,128)(2,1)}, u32[]{:S(2)}, u32[]{:S(2)}) async-start(bf16[8,128,1024]{2,1,0:T(8,128)(2,1)} %stack.2), calls=%async_computation | async-start | bytes 4194304 | tf_op jit(solution)/shard_map/all_to_all | solution.py:22
  15.1 42.3 %all-gather.2.cloned.1.call-start = ((), (), s32[]{:S(2)}) async-start(), calls=%async_computation.1 | async-start | bytes 1966080 | tf_op jit(solution)/shard_map/all_gather | solution.py:14
  45.7 1.3 %copy-start.1 = (bf16[1024,1024]{1,0:T(8,128)(2,1)}, bf16[1024,1024]{1,0:T(8,128)(2,1)S(1)}, u32[]{:S(2)}) copy-start(bf16[1024,1024]{1,0:T(8,128)(2,1)S(1)} %convolution_convert_fusion) | copy-start | bytes 6291460
  57.4 4.8 %copy-start.2 = (bf16[1024,1024]{1,0:T(8,128)(2,1)S(1)}, bf16[1024,1024]{1,0:T(8,128)(2,1)}, u32[]{:S(2)}) copy-start(bf16[1024,1024]{1,0:T(8,128)(2,1)} %copy-done.1) | copy-start | bytes 6291460
  57.4 4.8 %copy-start.3 = (f32[768,1024]{1,0:T(8,128)S(1)}, f32[768,1024]{1,0:T(8,128)}, u32[]{:S(2)}) copy-start(f32[768,1024]{1,0:T(8,128)} %param.5) | copy-start | bytes 9437188
Sparse Core Ops, SparseCore 0:
  17.4 39.9 all-gather.1
